TPU v7x, 256 devices: a whole 4x4x8 slice. The times are simulated.
256 devices in a mesh: gx: 8 (over z), gy: 16 (over y, x), gz: 2 (over core).
Axes of the slice: x: 4, y: 4, z: 8, core: 2. Of those that a mesh axis runs over, the one named last changes fastest.
Arguments:
- tensor: float32 [1024, 1024, 256], P('gx', 'gy', 'gz'), may hold values from -60 to 60
- factor_a: float32 [1024, 64], P(('gx', 'gy', 'gz')), may hold values from -6 to 6
- factor_b: float32 [1024, 64], P(('gy', 'gx', 'gz')), may hold values from -6 to 6
- factor_c: float32 [256, 64], P(('gz', 'gx', 'gy')), may hold values from -6 to 6
Outputs:
- slope_a: float32 [1024, 64], P(('gx', 'gy', 'gz'))
- slope_b: float32 [1024, 64], P(('gy', 'gx', 'gz'))
- slope_c: float32 [256, 64], P(('gz', 'gx', 'gy'))
All inputs are finite; a program needn't handle non-finite values.
Results may differ from a plain program's by a relative error of at most 0.0003.
Values sent between devices are 32-bit elements; how exact they have to be, the bound alone decides.
No kernel may reach another device: no remote copies, remote signals or barrier semaphores. Data moves between devices by JAX's collectives and lax.ppermute only.
A program may use at most 64 MiB of HBM per device.

v0:
```python
import jax
import jax.numpy as jnp
from jax import lax
from jax.sharding import PartitionSpec as P

STEPS = 2
step_size = 0.1


def gram_local(matrix):
    return jnp.dot(
        matrix.T, matrix, precision=lax.Precision.HIGHEST, preferred_element_type=jnp.float32
    )


def gather_blocks(own_a, own_b, own_c):
    block_a = lax.all_gather(own_a, ("gy", "gz"), axis=0, tiled=True)
    block_b = lax.all_gather(own_b, ("gx", "gz"), axis=0, tiled=True)
    block_c = lax.all_gather(own_c, ("gx", "gy"), axis=0, tiled=True)
    return (block_a, block_b, block_c)


def gram_sums(own_a, own_b, own_c):
    gram_a, gram_b, gram_c = lax.psum(
        (gram_local(own_a), gram_local(own_b), gram_local(own_c)), ("gx", "gy", "gz")
    )
    return (gram_a, gram_b, gram_c)


def partials(tensor, block_a, block_b, block_c):
    highest = lax.Precision.HIGHEST
    along_k = jnp.einsum("ijk,kr->jri", tensor, block_c, precision=highest)
    moment_a = jnp.einsum("jri,jr->ir", along_k, block_b, precision=highest)
    moment_b = jnp.einsum("jri,ir->jr", along_k, block_a, precision=highest)
    along_i = jnp.einsum("ijk,ir->rjk", tensor, block_a, precision=highest)
    moment_c = jnp.einsum("rjk,jr->kr", along_i, block_b, precision=highest)
    return (moment_a, moment_b, moment_c)


def slopes(first, second, third, moment_a, moment_b, moment_c, grams, counts):
    highest = lax.Precision.HIGHEST
    gram_a, gram_b, gram_c = grams
    count_i, count_j, count_k = counts
    slope_a = (jnp.dot(first, gram_b * gram_c, precision=highest) - moment_a) / (count_j * count_k)
    slope_b = (jnp.dot(second, gram_a * gram_c, precision=highest) - moment_b) / (count_i * count_k)
    slope_c = (jnp.dot(third, gram_a * gram_b, precision=highest) - moment_c) / (count_i * count_j)
    return (slope_a, slope_b, slope_c)


def shards(tensor, factor_a, factor_b, factor_c):
    counts = (
        float(tensor.shape[0] * lax.axis_size("gx")),
        float(tensor.shape[1] * lax.axis_size("gy")),
        float(tensor.shape[2] * lax.axis_size("gz")),
    )
    own_a, own_b, own_c = (factor_a, factor_b, factor_c)
    for round_index in range(STEPS):
        block_a, block_b, block_c = gather_blocks(own_a, own_b, own_c)
        grams = gram_sums(own_a, own_b, own_c)
        moment_a, moment_b, moment_c = partials(tensor, block_a, block_b, block_c)
        moment_a = lax.psum_scatter(moment_a, ("gy", "gz"), scatter_dimension=0, tiled=True)
        moment_b = lax.psum_scatter(moment_b, ("gx", "gz"), scatter_dimension=0, tiled=True)
        moment_c = lax.psum_scatter(moment_c, ("gx", "gy"), scatter_dimension=0, tiled=True)
        slope_a, slope_b, slope_c = slopes(
            own_a, own_b, own_c, moment_a, moment_b, moment_c, grams, counts
        )
        if round_index + 1 < STEPS:
            own_a = own_a - step_size * slope_a
            own_b = own_b - step_size * slope_b
            own_c = own_c - step_size * slope_c
    return (slope_a, slope_b, slope_c)


def solution(mesh):
    placed = (
        P("gx", "gy", "gz"),
        P(("gx", "gy", "gz"), None),
        P(("gy", "gx", "gz"), None),
        P(("gz", "gx", "gy"), None),
    )
    return jax.shard_map(
        shards,
        mesh=mesh,
        in_specs=placed,
        out_specs=(
            P(("gx", "gy", "gz"), None),
            P(("gy", "gx", "gz"), None),
            P(("gz", "gx", "gy"), None),
        ),
        check_vma=False,
    )
```

profile of v0, /device:TPU:1, one launch (start us, length us, event | category | flops | bytes accessed | tf_op | source)
XLA Modules:
  0.0 1523.7 jit_solution(15160832706329019883)
XLA Ops:
  7.2 1.0 fusion.29
  8.2 21.6 %all-gather.1 = f32[16,4,64]{2,1,0:T(4,128)S(1)} all-gather(f32[1,4,64]{2,1,0:T(4,128)} %bitcast.117), channel_id=1, replica_groups=mesh['gx'=8,'gy'=16,'gz'=2] {'gx','gz'}, dimensions={0}, use_global_device_ids=true | all-gather | bytes 17408 | tf_op jit(solution)/shard_map/all_gather | solution.py:18
  29.8 284.8 %all-gather = f32[128,1,64]{2,1,0:T(1,128)S(1)} all-gather(f32[1,1,64]{2,1,0:T(1,128)} %bitcast.121), channel_id=1, replica_groups=mesh['gx'=8,'gy'=16,'gz'=2] {'gx','gy'}, dimensions={0}, use_global_device_ids=true | all-gather | bytes 33024 | tf_op jit(solution)/shard_map/all_gather | solution.py:19
  314.7 1.0 fusion.30
  315.7 77.7 %all-gather.2 = f32[32,4,64]{2,1,0:T(4,128)S(1)} all-gather(f32[1,4,64]{2,1,0:T(4,128)} %bitcast.118), channel_id=1, replica_groups=mesh['gx'=8,'gy'=16,'gz'=2] {'gy','gz'}, dimensions={0}, use_global_device_ids=true | all-gather | bytes 33792 | tf_op jit(solution)/shard_map/all_gather | solution.py:17
  393.5 9.2 fusion.9
  402.8 0.6 multiply_reduce_fusion.3
  403.4 42.5 %all-reduce.1 = f32[64,64]{1,0:T(8,128)S(1)} all-reduce(f32[64,64]{1,0:T(8,128)S(1)} %bitcast.113), channel_id=3, replica_groups=mesh['gx'=8,'gy'=16,'gz'=2] {'gx','gz'}, use_global_device_ids=true, to_apply=%region_4.0.clone | all-reduce | flops 4096 | bytes 32768
  446.1 0.6 dynamic-slice.2
  447.3 76.9 %all-reduce.7 = (f32[64,64]{1,0:T(8,128)S(1)}, f32[64,64]{1,0:T(8,128)S(1)}, f32[64,64]{1,0:T(8,128)S(1)}) all-reduce(f32[64,64]{1,0:T(8,128)S(1)} %fusion.29, f32[64,64]{1,0:T(8,128)S(1)} %broadcast_multiply_fusion.1, f32[64,64]{1,0:T(8,128)S(1)} %fusion.30), channel_id=1, replica_groups=mesh['gx'=8,'gy'=16,'gz'=2] {'gx','gy','gz'}, use_global_device_ids=true, to_apply=%region_0.0 | all-reduce | flops 12288 | bytes 98304 | tf_op jit(solution)/shard_map/psum | solution.py:24
  524.4 17.3 %all-gather.3 = f32[16,4,64]{2,1,0:T(4,128)S(1)} all-gather(f32[1,4,64]{2,1,0:T(4,128)S(1)} %bitcast.115), channel_id=1, replica_groups=mesh['gx'=8,'gy'=16,'gz'=2] {'gx','gz'}, dimensions={0}, use_global_device_ids=true | all-gather | bytes 17408 | tf_op jit(solution)/shard_map/all_gather | solution.py:18
  541.8 0.6 dynamic-slice
  543.2 119.2 %all-reduce = f32[128,64]{1,0:T(8,128)S(1)} all-reduce(f32[128,64]{1,0:T(8,128)S(1)} %bitcast.111), channel_id=2, replica_groups=mesh['gx'=8,'gy'=16,'gz'=2] {'gy','gz'}, use_global_device_ids=true, to_apply=%region_2.0.clone | all-reduce | flops 8192 | bytes 65536
  662.5 26.8 %all-gather.5 = f32[32,4,64]{2,1,0:T(4,128)S(1)} all-gather(f32[1,4,64]{2,1,0:T(4,128)S(1)} %bitcast.116), channel_id=1, replica_groups=mesh['gx'=8,'gy'=16,'gz'=2] {'gy','gz'}, dimensions={0}, use_global_device_ids=true | all-gather | bytes 33792 | tf_op jit(solution)/shard_map/all_gather | solution.py:17
  689.3 7.2 fusion
  696.5 2.4 multiply_reduce_fusion
  698.9 0.7 copy.52
  699.6 7.2 fusion.2
  706.8 2.4 multiply_reduce_fusion.2
  709.3 0.7 copy.33
  710.5 0.6 dynamic-slice.4
  711.2 203.8 %all-reduce.11.cloned.1.call-done = (f32[128,64]{1,0:T(8,128)}, f32[128,64]{1,0:T(8,128)}) async-done(((f32[128,64]{1,0:T(8,128)}, f32[128,64]{1,0:T(8,128)}), (f32[128,64]{1,0:T(8,128)}, f32[128,64]{1,0:T(8,128)})) %all-reduce.11.cloned.1.call-update) | async-done | bytes 65552
  914.9 1.5 fusion.19
  916.5 285.2 %all-gather.4 = f32[128,1,64]{2,1,0:T(1,128)S(1)} all-gather(f32[1,1,64]{2,1,0:T(1,128)S(1)} %bitcast.120), channel_id=1, replica_groups=mesh['gx'=8,'gy'=16,'gz'=2] {'gx','gy'}, dimensions={0}, use_global_device_ids=true | all-gather | bytes 33024 | tf_op jit(solution)/shard_map/all_gather | solution.py:19
  1201.6 9.3 fusion.8
  1210.9 0.6 multiply_reduce_fusion.1
  1211.5 103.3 %all-reduce.4 = f32[64,64]{1,0:T(8,128)S(1)} all-reduce(f32[64,64]{1,0:T(8,128)S(1)} %bitcast.114), channel_id=6, replica_groups=mesh['gx'=8,'gy'=16,'gz'=2] {'gx','gz'}, use_global_device_ids=true, to_apply=%region_10.0.clone | all-reduce | flops 4096 | bytes 32768
  1314.9 121.7 %all-reduce.3 = f32[128,64]{1,0:T(8,128)S(1)} all-reduce(f32[128,64]{1,0:T(8,128)S(1)} %bitcast.112), channel_id=5, replica_groups=mesh['gx'=8,'gy'=16,'gz'=2] {'gy','gz'}, use_global_device_ids=true, to_apply=%region_8.0.clone | all-reduce | flops 8192 | bytes 65536
  1436.6 76.7 %all-reduce.6 = (f32[64,64]{1,0:T(8,128)S(1)}, f32[64,64]{1,0:T(8,128)S(1)}, f32[64,64]{1,0:T(8,128)S(1)}) all-reduce(f32[64,64]{1,0:T(8,128)S(1)} %fusion.31, f32[64,64]{1,0:T(8,128)S(1)} %broadcast_multiply_fusion, f32[64,64]{1,0:T(8,128)S(1)} %fusion.32), channel_id=1, replica_groups=mesh['gx'=8,'gy'=16,'gz'=2] {'gx','gy','gz'}, use_global_device_ids=true, to_apply=%region_5.0 | all-reduce | flops 12288 | bytes 98304 | tf_op jit(solution)/shard_map/psum | solution.py:24
  1513.4 2.0 fusion.20
  1515.4 0.7 fusion.10
  1516.1 0.7 fusion.11
  (26 shorter events, 1.5 us)
Async XLA Ops:
  7.2 907.8 %all-reduce.11.cloned.1.call-start = ((), (), s32[]{:S(2)}) async-start(), calls=%async_computation | async-start | bytes 262144
  402.8 43.2 %copy-start.2 = (f32[1,64]{1,0:T(1,128)S(1)}, f32[1,64]{1,0:T(1,128)}, u32[]{:S(2)}) copy-start(f32[1,64]{1,0:T(1,128)} %param.7) | copy-start | bytes 772
  402.8 43.3 %copy-start.5 = (u32[256]{0:T(256)S(1)}, u32[256]{0:T(256)}, u32[]{:S(2)}) copy-start(u32[256]{0:T(256)} %constant.32) | copy-start | bytes 3076
  402.8 121.5 %copy-start = (f32[4,64]{1,0:T(4,128)S(1)}, f32[4,64]{1,0:T(4,128)}, u32[]{:S(2)}) copy-start(f32[4,64]{1,0:T(4,128)} %param.6) | copy-start | bytes 3076
  402.8 139.0 %copy-start.4 = (u32[256]{0:T(256)S(1)}, u32[256]{0:T(256)}, u32[]{:S(2)}) copy-start(u32[256]{0:T(256)} %constant.28) | copy-start | bytes 3076
  402.8 259.5 %copy-start.1 = (f32[4,64]{1,0:T(4,128)S(1)}, f32[4,64]{1,0:T(4,128)}, u32[]{:S(2)}) copy-start(f32[4,64]{1,0:T(4,128)} %param.5) | copy-start | bytes 3076
  706.8 3.7 copy-start.3
Sparse Core Ops, SparseCore 0:
  710.1 204.7 all-reduce.10
where the time goes:
time: 1520 us
  blocking collectives  1250 us (82%)
  waiting for transfers between devices  204 us (13%)
  matrix products  40.5 us (3%)
  between operations  15.5 us (1%)
    all_gather x2, blocking collectives, gather_blocks(): block_c = lax.all_gather(own_c, ('gx', 'gy'), axis=0, tiled=True)  570 us
    unnamed x4, blocking collectives  387 us
    unnamed x2, waiting for transfers between devices  204 us
    psum x2, blocking collectives, gram_sums(): lax.psum((gram_local(own_a), gram_local(own_b), gram_local(own_c)), ('gx'...  154 us
    all_gather x2, blocking collectives, gather_blocks(): block_a = lax.all_gather(own_a, ('gy', 'gz'), axis=0, tiled=True)  105 us
    all_gather x2, blocking collectives, gather_blocks(): block_b = lax.all_gather(own_b, ('gx', 'gz'), axis=0, tiled=True)  39 us
  transfers between devices with their start and end apart: 1, of which 1 were waited for; matrix products, arithmetic and copies ran while one was open for 0% of the time, Pallas kernels for 0%

commit v1 on v0

--- a/solution.py
+++ b/solution.py
@@ -5,6 +5,7 @@
 
 STEPS = 2
 step_size = 0.1
+pair_runs = lambda w_in: lax.psum(lax.psum(w_in, "gx"), ("gy", "gz"))
 
 
 def gram_local(matrix):
@@ -21,9 +22,7 @@
 
 
 def gram_sums(own_a, own_b, own_c):
-    gram_a, gram_b, gram_c = lax.psum(
-        (gram_local(own_a), gram_local(own_b), gram_local(own_c)), ("gx", "gy", "gz")
-    )
+    gram_a, gram_b, gram_c = pair_runs((gram_local(own_a), gram_local(own_b), gram_local(own_c)))
     return (gram_a, gram_b, gram_c)
 
 

time: 1520 us -> 1270 us (0.84)
  blocking collectives: 1250 us -> 914 us
  waiting for transfers between devices: 204 us -> 287 us
    unnamed x4 -> x2, blocking collectives: 387 us -> 155 us
    psum x2, blocking collectives: 154 us -> 43.9 us  [pair_runs = lambda w_in: lax.psum(lax.psum(w_in, 'gx'), ('gy', 'gz'))]
    psum x0 -> x2, waiting for transfers between devices: none -> 83.3 us  [pair_runs = lambda w_in: lax.psum(lax.psum(w_in, 'gx'), ('gy', 'gz'))]
    unnamed x2 -> x4, waiting for transfers between devices: 204 us -> 204 us
  transfers between devices with their start and end apart: 1 -> 3, of which waited for: 1 -> 3; matrix products, arithmetic and copies ran while one was open for 0% -> 1% of each run, Pallas kernels for 0% -> 0%
where the time goes in v1:
time: 1270 us
  blocking collectives  914 us (72%)
  waiting for transfers between devices  287 us (23%)
  matrix products  43.7 us (3%)
  between operations  15.2 us (1%)
    all_gather x2, blocking collectives, gather_blocks(): block_c = lax.all_gather(own_c, ('gx', 'gy'), axis=0, tiled=True)  570 us
    unnamed x4, waiting for transfers between devices  204 us
    unnamed x2, blocking collectives  155 us
    all_gather x2, blocking collectives, gather_blocks(): block_a = lax.all_gather(own_a, ('gy', 'gz'), axis=0, tiled=True)  107 us
    psum x2, waiting for transfers between devices, pair_runs = lambda w_in: lax.psum(lax.psum(w_in, 'gx'), ('gy', 'gz'))  83.3 us
    psum x2, blocking collectives, pair_runs = lambda w_in: lax.psum(lax.psum(w_in, 'gx'), ('gy', 'gz'))  43.9 us
    all_gather x2, blocking collectives, gather_blocks(): block_b = lax.all_gather(own_b, ('gx', 'gz'), axis=0, tiled=True)  39 us
  transfers between devices with their start and end apart: 3, of which 3 were waited for; matrix products, arithmetic and copies ran while one was open for 1% of the time, Pallas kernels for 0%

profile of v1, /device:TPU:1, one launch (start us, length us, event | category | flops | bytes accessed | tf_op | source)
XLA Modules:
  0.0 1272.3 jit_solution(5839829745743680472)
XLA Ops:
  7.2 0.8 broadcast_multiply_fusion.1
  8.0 1.0 fusion.29
  9.0 21.6 %all-gather.1 = f32[16,4,64]{2,1,0:T(4,128)S(1)} all-gather(f32[1,4,64]{2,1,0:T(4,128)} %bitcast.117), channel_id=1, replica_groups=mesh['gx'=8,'gy'=16,'gz'=2] {'gx','gz'}, dimensions={0}, use_global_device_ids=true | all-gather | bytes 17408 | tf_op jit(solution)/shard_map/all_gather | solution.py:19
  30.6 1.0 fusion.30
  31.6 284.8 %all-gather = f32[128,1,64]{2,1,0:T(1,128)S(1)} all-gather(f32[1,1,64]{2,1,0:T(1,128)} %bitcast.122), channel_id=1, replica_groups=mesh['gx'=8,'gy'=16,'gz'=2] {'gx','gy'}, dimensions={0}, use_global_device_ids=true | all-gather | bytes 33024 | tf_op jit(solution)/shard_map/all_gather | solution.py:20
  316.5 9.2 fusion.9
  325.7 0.7 copy.21
  326.4 21.8 %all-reduce.10 = (f32[64,64]{1,0:T(8,128)}, f32[64,64]{1,0:T(8,128)}, f32[64,64]{1,0:T(8,128)}) all-reduce(f32[64,64]{1,0:T(8,128)S(1)} %fusion.29, f32[64,64]{1,0:T(8,128)S(1)} %broadcast_multiply_fusion.1, f32[64,64]{1,0:T(8,128)S(1)} %fusion.30), channel_id=1, replica_groups=mesh['gx'=8,'gy'=16,'gz'=2] {'gx'}, use_global_device_ids=true, to_apply=%region_0.0 | all-reduce | flops 12288 | bytes 98304 | tf_op jit(solution)/shard_map/psum | solution.py:8
  348.4 83.8 %all-gather.2 = f32[32,4,64]{2,1,0:T(4,128)S(1)} all-gather(f32[1,4,64]{2,1,0:T(4,128)S(1)} %bitcast.118), channel_id=1, replica_groups=mesh['gx'=8,'gy'=16,'gz'=2] {'gy','gz'}, dimensions={0}, use_global_device_ids=true | all-gather | bytes 33792 | tf_op jit(solution)/shard_map/all_gather | solution.py:18
  432.2 7.2 fusion.2
  439.5 2.4 multiply_reduce_fusion.2
  445.6 0.7 copy.33
  446.3 44.4 %all-reduce.1 = f32[64,64]{1,0:T(8,128)S(1)} all-reduce(f32[64,64]{1,0:T(8,128)S(1)} %bitcast.113), channel_id=3, replica_groups=mesh['gx'=8,'gy'=16,'gz'=2] {'gx','gz'}, use_global_device_ids=true, to_apply=%region_7.0.clone | all-reduce | flops 4096 | bytes 32768
  490.8 23.5 %all-reduce.19.cloned.1.call-done = (f32[64,64]{1,0:T(8,128)}, f32[64,64]{1,0:T(8,128)}, f32[128,64]{1,0:T(8,128)}, f32[64,64]{1,0:T(8,128)}) async-done(((f32[64,64]{1,0:T(8,128)}, f32[64,64]{1,0:T(8,128)}, f32[128,64]{1,0:T(8,128)}, f32[64,64]{1,0:T(8,128)}), (f32[64,64]{1,0:T(8,128)}, f32[64,64]{1,0:T(8,128)}, f32[128,64]{1,0:T(8,128)}, f32[64,64]{1,0:T(8,128)})) %all-reduce.19.cloned.1.call-update) | async-done | bytes 81936 | tf_op jit(solution)/shard_map/psum | solution.py:8
  514.2 0.9 fusion.14
  515.1 17.4 %all-gather.3 = f32[16,4,64]{2,1,0:T(4,128)S(1)} all-gather(f32[1,4,64]{2,1,0:T(4,128)S(1)} %bitcast.116), channel_id=1, replica_groups=mesh['gx'=8,'gy'=16,'gz'=2] {'gx','gz'}, dimensions={0}, use_global_device_ids=true | all-gather | bytes 17408 | tf_op jit(solution)/shard_map/all_gather | solution.py:19
  532.6 0.9 fusion.17
  533.8 23.0 %all-gather.5 = f32[32,4,64]{2,1,0:T(4,128)S(1)} all-gather(f32[1,4,64]{2,1,0:T(4,128)S(1)} %bitcast.115), channel_id=1, replica_groups=mesh['gx'=8,'gy'=16,'gz'=2] {'gy','gz'}, dimensions={0}, use_global_device_ids=true | all-gather | bytes 33792 | tf_op jit(solution)/shard_map/all_gather | solution.py:18
  556.8 7.2 fusion
  564.0 2.4 multiply_reduce_fusion
  566.5 0.7 copy.52
  567.6 204.0 %all-reduce.15.cloned.1.call-done = (f32[128,64]{1,0:T(8,128)}, f32[128,64]{1,0:T(8,128)}) async-done(((f32[128,64]{1,0:T(8,128)}, f32[128,64]{1,0:T(8,128)}), (f32[128,64]{1,0:T(8,128)}, f32[128,64]{1,0:T(8,128)})) %all-reduce.15.cloned.1.call-update) | async-done | bytes 65552
  771.5 1.5 fusion.19
  773.1 285.0 %all-gather.4 = f32[128,1,64]{2,1,0:T(1,128)S(1)} all-gather(f32[1,1,64]{2,1,0:T(1,128)S(1)} %bitcast.120), channel_id=1, replica_groups=mesh['gx'=8,'gy'=16,'gz'=2] {'gx','gy'}, dimensions={0}, use_global_device_ids=true | all-gather | bytes 33024 | tf_op jit(solution)/shard_map/all_gather | solution.py:20
  1058.0 9.2 fusion.8
  1067.3 0.7 copy.40
  1068.0 22.1 %all-reduce.9 = (f32[64,64]{1,0:T(8,128)}, f32[64,64]{1,0:T(8,128)}, f32[64,64]{1,0:T(8,128)}) all-reduce(f32[64,64]{1,0:T(8,128)S(1)} %fusion.31, f32[64,64]{1,0:T(8,128)S(1)} %broadcast_multiply_fusion, f32[64,64]{1,0:T(8,128)S(1)} %fusion.32), channel_id=1, replica_groups=mesh['gx'=8,'gy'=16,'gz'=2] {'gx'}, use_global_device_ids=true, to_apply=%region_8.0 | all-reduce | flops 12288 | bytes 98304 | tf_op jit(solution)/shard_map/psum | solution.py:8
  1090.8 110.1 %all-reduce.4 = f32[64,64]{1,0:T(8,128)S(1)} all-reduce(f32[64,64]{1,0:T(8,128)S(1)} %bitcast.114), channel_id=6, replica_groups=mesh['gx'=8,'gy'=16,'gz'=2] {'gx','gz'}, use_global_device_ids=true, to_apply=%region_16.0.clone | all-reduce | flops 4096 | bytes 32768
  1200.9 59.8 %all-reduce.17.cloned.1.call-done = (f32[64,64]{1,0:T(8,128)}, f32[64,64]{1,0:T(8,128)}, f32[128,64]{1,0:T(8,128)}, f32[64,64]{1,0:T(8,128)}) async-done(((f32[64,64]{1,0:T(8,128)}, f32[64,64]{1,0:T(8,128)}, f32[128,64]{1,0:T(8,128)}, f32[64,64]{1,0:T(8,128)}), (f32[64,64]{1,0:T(8,128)}, f32[64,64]{1,0:T(8,128)}, f32[128,64]{1,0:T(8,128)}, f32[64,64]{1,0:T(8,128)})) %all-reduce.17.cloned.1.call-update) | async-done | bytes 81936 | tf_op jit(solution)/shard_map/psum | solution.py:8
  1260.7 1.5 fusion.10
  1262.2 2.1 fusion.20
  1264.3 1.5 fusion.11
  (34 shorter events, 4.0 us)
Async XLA Ops:
  7.2 507.0 %all-reduce.19.cloned.1.call-start = ((), (), s32[]{:S(2)}) async-start(), calls=%async_computation.2 | async-start | bytes 327680 | tf_op jit(solution)/shard_map/psum | solution.py:8
  316.5 31.9 %copy-start.3 = (f32[4,64]{1,0:T(4,128)S(1)}, f32[4,64]{1,0:T(4,128)}, u32[]{:S(2)}) copy-start(f32[4,64]{1,0:T(4,128)} %param.5) | copy-start | bytes 3076
  348.3 423.3 %all-reduce.15.cloned.1.call-start = ((), (), s32[]{:S(2)}) async-start(), calls=%async_computation | async-start | bytes 262144
  439.5 3.1 copy-start.7
  439.5 3.7 copy-start.6
  439.5 4.3 copy-start.5
  439.5 74.7 %copy-start.2 = (f32[4,64]{1,0:T(4,128)S(1)}, f32[4,64]{1,0:T(4,128)}, u32[]{:S(2)}) copy-start(f32[4,64]{1,0:T(4,128)} %param.6) | copy-start | bytes 3076
  564.0 207.5 %copy-start = (f32[64,64]{1,0:T(8,128)S(1)}, f32[64,64]{1,0:T(8,128)}, u32[]{:S(2)}) copy-start(f32[64,64]{1,0:T(8,128)} %get-tuple-element.9) | copy-start | bytes 49156
  564.0 207.5 %copy-start.1 = (f32[64,64]{1,0:T(8,128)S(1)}, f32[64,64]{1,0:T(8,128)}, u32[]{:S(2)}) copy-start(f32[64,64]{1,0:T(8,128)} %get-tuple-element.12) | copy-start | bytes 49156
  564.0 207.5 %copy-start.4 = (f32[1,64]{1,0:T(1,128)S(1)}, f32[1,64]{1,0:T(1,128)}, u32[]{:S(2)}) copy-start(f32[1,64]{1,0:T(1,128)} %param.7) | copy-start | bytes 772
  567.2 693.5 %all-reduce.17.cloned.1.call-start = ((), (), s32[]{:S(2)}) async-start(), calls=%async_computation.1 | async-start | bytes 327680 | tf_op jit(solution)/shard_map/psum | solution.py:8
Sparse Core Ops, SparseCore 0:
  348.4 165.7 all-reduce.18
  567.3 204.1 all-reduce.14
  1090.3 170.3 all-reduce.16
